TPU v7x, 32 devices: a whole 2x2x4 slice. The times are simulated.
32 devices in a mesh: region: 4 (over z), enc: 8 (over y, x, core).
Axes of the slice: x: 2, y: 2, z: 4, core: 2. Of those that a mesh axis runs over, the one named last changes fastest.
Arguments:
- pixels: bfloat16 [256, 48, 4096], P(('region', 'enc')), may hold values from -6 to 6
- feature_grad: bfloat16 [256, 96, 4096], P(('region', 'enc')), may hold values from -0.0046691895 to 0.0046691895
- tissue_count: int32 [32], P(('region', 'enc')), may hold values from 1 to 8, as said below
- stem_weight: bfloat16 [96, 48], replicated, may hold values from -0.875 to 0.875
- stem_gain: float32 [96], replicated, may hold values from 0.5 to 1.5
- stem_shift: float32 [96], replicated, may hold values from -3 to 3
- depth_kernel: float32 [96, 49], replicated, may hold values from -0.875 to 0.875
- block_gain: float32 [96], replicated, may hold values from 0.5 to 1.5
- expand_weight: bfloat16 [384, 96], replicated, may hold values from -0.625 to 0.625
- expand_bias: float32 [384], replicated, may hold values from -3 to 3
- reduce_weight: bfloat16 [96, 384], replicated, may hold values from -0.3125 to 0.3125
- layer_scale: float32 [96], replicated, may hold values from 0.5 to 1.5
Outputs:
- features: bfloat16 [256, 96, 4096], P(('region', 'enc'))
- grad_stem: float32 [96, 48], replicated
- grad_gain: float32 [96], replicated
- grad_shift: float32 [96], replicated
- grad_kernel: float32 [96, 49], replicated
- grad_norm: float32 [96], replicated
- grad_expand: float32 [384, 96], replicated
- grad_bias: float32 [384], replicated
- grad_reduce: float32 [96, 384], replicated
- grad_scale: float32 [96], replicated
Inputs may be any that keep to these rules, and one draw needn't show every extreme that they name: `tissue_count`: the tissue tiles of a device fill its first slots; the other slots are unused.
All inputs are finite; a program needn't handle non-finite values.
Results may differ from a plain program's by a relative error of at most 0.015.
Values may be sent and summed in bfloat16 or wider, within the bound.
A program may use at most 256 MiB of HBM per device.

v0:
```python
import jax
import jax.numpy as jnp
import numpy as np
from jax import lax
from jax.experimental import pallas as pl
from jax.experimental.pallas import tpu as pltpu
from jax.sharding import PartitionSpec as P

SIDE = 64
KSIZE = 7
EPS = 1e-06
LANES = 128
CHUNK = 512
PAD = 2
BLOCKS = 10
EXACT = lax.Precision.HIGHEST
MESH = pl.DeviceIdType.MESH

f32 = jnp.float32
bf16 = jnp.bfloat16


def dot(a, b, dims=((1,), (0,))):
    return lax.dot_general(a, b, (dims, ((), ())), preferred_element_type=f32)


def wide(value, times):
    return jnp.concatenate([value] * times, axis=1)


def fold(value):
    total = value[:, :LANES]
    for at in range(LANES, value.shape[1], LANES):
        total = total + value[:, at : at + LANES]
    return total


def unit(values):
    centre = jnp.mean(values, axis=0, keepdims=True)
    shifted = values - centre
    spread = jnp.mean(jnp.square(shifted), axis=0, keepdims=True)
    scale = lax.rsqrt(spread + EPS)
    return shifted * scale, scale


def unit_back(grad, hat, scale):
    first = jnp.mean(grad, axis=0, keepdims=True)
    second = jnp.mean(grad * hat, axis=0, keepdims=True)
    return scale * (grad - first - hat * second)


def gelu_both(x):
    decay = jnp.exp(x * x * -0.5)
    t = 1.0 / (1.0 + jnp.abs(x) * (0.3275911 * 0.7071067811865476))
    poly = t * (
        0.5 * 0.254829592
        + t
        * (
            0.5 * -0.284496736
            + t * (0.5 * 1.421413741 + t * (0.5 * -1.453152027 + t * (0.5 * 1.061405429)))
        )
    )
    tail = poly * decay
    cdf = jnp.where(x >= 0, 1.0 - tail, tail)
    return x * cdf, cdf + x * (decay * 0.3989422804014327)


def body(
    count_ref, pix_ref, grad_ref, ws_ref, gain_ref, shift_ref, norm_ref, scale_ref, kernel_ref,
    we_in_ref, bias_ref, wr_ref, place_ref, place_back_ref, pick_ref, feat_ref, sums_ref, base_s,
    mix_s, ex_s, dh_s, hid_s, de_s, par_ref, we_ref, wet_ref, wrt_ref, taps_ref, back_ref,
    dws_ref, dvec_ref, dwe_ref, dwr_ref, dk_ref,
):
    phase = pl.program_id(0)
    slot = pl.program_id(1)
    slots = pl.num_programs(1)
    live = slot < count_ref[0]
    channels, area = grad_ref.shape[1:]
    pairs = area // LANES
    per = CHUNK // LANES
    chunks = area // CHUNK
    hidden = we_ref.shape[0]
    rows = base_s.shape[1] // channels

    row_at = lax.broadcasted_iota(jnp.int32, (SIDE, LANES), 0)
    lane_at = lax.broadcasted_iota(jnp.int32, (SIDE, LANES), 1) % SIDE
    near = jnp.abs(row_at - lane_at) <= KSIZE // 2
    near_mirrored = jnp.abs(SIDE - 1 - row_at - lane_at) <= KSIZE // 2
    row_all = lax.broadcasted_iota(jnp.int32, (LANES, LANES), 0)
    lane_all = lax.broadcasted_iota(jnp.int32, (LANES, LANES), 1)
    same = row_all // SIDE == lane_all // SIDE
    mirror = (same & (row_all % SIDE + lane_all % SIDE == SIDE - 1)).astype(f32).astype(bf16)

    def read(ref, chunk):
        return jnp.concatenate(
            [
                ref[PAD + chunk * per + at, pl.ds(slot, channels, stride=rows), :]
                for at in range(per)
            ],
            axis=1,
        )

    def write(ref, chunk, value):
        for at in range(per):
            ref[PAD + chunk * per + at, pl.ds(slot, channels, stride=rows), :] = value[
                :, at * LANES : (at + 1) * LANES
            ]

    def param(at):
        return wide(par_ref[at], per)

    def toeplitz(ref, c):
        blocks = []
        for m in range(BLOCKS):
            row = jnp.broadcast_to(ref[c, m : m + 1, :], (SIDE, LANES))
            turned = pltpu.roll(row, 0, 1, stride=1, stride_axis=0)
            blocks.append(jnp.where(near, turned, 0.0).astype(bf16))
        return jnp.concatenate(blocks, axis=0)

    def gathered(ref, c):
        at = pl.multiple_of(c * rows, rows)
        full = ref[:, pl.ds(at, rows), :]
        even = full.reshape((pairs + 2 * PAD) * rows, LANES).astype(bf16)
        odd = full[1 : pairs + 3].reshape((pairs + 2) * rows, LANES).astype(bf16)
        size = pairs * rows
        return jnp.concatenate(
            [
                even[:size],
                odd[:size],
                even[2 * rows : 2 * rows + size],
                odd[2 * rows : 2 * rows + size],
                even[4 * rows : 4 * rows + size],
            ],
            axis=1,
        )

    @pl.when((phase == 0) & (slot == 0))
    def _():
        base_s[...] = jnp.zeros(base_s.shape, f32)
        mix_s[...] = jnp.zeros(mix_s.shape, f32)
        dws_ref[...] = jnp.zeros(dws_ref.shape, f32)
        dvec_ref[...] = jnp.zeros(dvec_ref.shape, f32)
        dwe_ref[...] = jnp.zeros(dwe_ref.shape, f32)
        dwr_ref[...] = jnp.zeros(dwr_ref.shape, f32)
        for at, ref in enumerate((gain_ref, shift_ref, norm_ref, scale_ref)):
            par_ref[at] = jnp.transpose(jnp.broadcast_to(ref[...], (LANES, channels)))
        kernel = kernel_ref[...].astype(bf16)
        for m in range(BLOCKS):
            taps_ref[:, m, :] = dot(kernel, place_ref[m])
            back_ref[:, m, :] = dot(kernel, place_back_ref[m])
        weight = we_in_ref[...].astype(f32)
        wet_ref[...] = jnp.transpose(weight).astype(bf16)
        wrt_ref[...] = jnp.transpose(wr_ref[...].astype(f32)).astype(bf16)
        bias = jnp.transpose(jnp.broadcast_to(bias_ref[...], (LANES, hidden)))
        high = bias.astype(bf16).astype(f32)
        middle = (bias - high).astype(bf16).astype(f32)
        low = bias - high - middle
        lane = lax.broadcasted_iota(jnp.int32, (hidden, LANES), 1)
        extra = jnp.where(
            lane == channels,
            high,
            jnp.where(lane == channels + 1, middle, jnp.where(lane == channels + 2, low, 0.0)),
        )
        we_ref[...] = extra.astype(bf16)
        we_ref[:, :channels] = we_in_ref[...]

    @pl.when((phase == 0) & live)
    def _():
        @pl.loop(0, chunks, unroll=4)
        def _(chunk):
            at = pl.multiple_of(chunk * CHUNK, CHUNK)
            out = dot(ws_ref[...], pix_ref[0, :, pl.ds(at, CHUNK)])
            hat, _ = unit(out)
            base = (hat * param(0) + param(1)).astype(bf16).astype(f32)
            write(base_s, chunk, base)

    @pl.when((phase == 1) & (slot == 0))
    def _():
        @pl.loop(0, channels, unroll=8)
        def _(c):
            out = dot(gathered(base_s, c), toeplitz(taps_ref, c))
            at = pl.multiple_of(c * rows, rows)
            mix_s[PAD : PAD + pairs, pl.ds(at, rows), :] = out.reshape(pairs, rows, LANES)

    @pl.when((phase == 1) & live)
    def _():
        @pl.loop(0, chunks, unroll=4)
        def _(chunk):
            at = pl.multiple_of(chunk * CHUNK, CHUNK)
            hat, scale = unit(read(mix_s, chunk))
            normed = (hat * param(2)).astype(bf16)
            normed = jnp.concatenate([normed, jnp.ones((LANES - channels, CHUNK), bf16)], axis=0)
            grad = grad_ref[0, :, pl.ds(at, CHUNK)]
            ex_s[...] = dot(we_ref[...], normed)
            dh_s[...] = dot(wrt_ref[...], (grad.astype(f32) * param(3)).astype(bf16))
            for h in range(0, hidden, 16):
                act, slope = gelu_both(ex_s[h : h + 16, :])
                hid_s[h : h + 16, :] = act.astype(bf16)
                de_s[h : h + 16, :] = (slope * dh_s[h : h + 16, :]).astype(bf16)
            reduced = dot(wr_ref[...], hid_s[...])
            feat_ref[0, :, pl.ds(at, CHUNK)] = (
                read(base_s, chunk) + param(3) * reduced
            ).astype(bf16)
            dwr_ref[...] += dot(grad, hid_s[...], ((1,), (1,)))
            dwe_ref[...] += dot(de_s[...], normed, ((1,), (1,)))
            dn = dot(wet_ref[...], de_s[...])
            dvec_ref[2] += fold(dn * hat)
            write(mix_s, chunk, unit_back(dn * param(2), hat, scale))

    @pl.when((phase == 1) & jnp.logical_not(live))
    def _():
        feat_ref[...] = jnp.zeros(feat_ref.shape, bf16)

    @pl.when((phase == 2) & (slot == 0))
    def _():
        @pl.loop(0, channels, unroll=8)
        def _(c):
            at = pl.multiple_of(c * rows, rows)
            grad = mix_s[PAD : PAD + pairs, pl.ds(at, rows), :]
            grad = grad.reshape(pairs * rows, LANES).astype(bf16)
            grad = dot(grad, mirror).astype(bf16)
            cross = dot(grad, gathered(base_s, c), ((0,), (0,)))
            for r in range(2):
                for k in range(BLOCKS // 2):
                    part = cross[r * SIDE : (r + 1) * SIDE, k * LANES : (k + 1) * LANES]
                    part = pltpu.roll(
                        jnp.where(near_mirrored, part, 0.0), 0, 1, stride=1, stride_axis=0
                    )
                    dk_ref[c, r * 5 + k : r * 5 + k + 1, :] = jnp.sum(
                        part, axis=0, keepdims=True
                    )
            out = dot(gathered(mix_s, c), toeplitz(back_ref, c))
            mix_s[PAD : PAD + pairs, pl.ds(at, rows), :] = out.reshape(pairs, rows, LANES)

    @pl.when((phase == 2) & live)
    def _():
        @pl.loop(0, chunks, unroll=4)
        def _(chunk):
            at = pl.multiple_of(chunk * CHUNK, CHUNK)
            pix = pix_ref[0, :, pl.ds(at, CHUNK)]
            hat, scale = unit(dot(ws_ref[...], pix))
            dbase = grad_ref[0, :, pl.ds(at, CHUNK)].astype(f32) + read(mix_s, chunk)
            dvec_ref[0] += fold(dbase * hat)
            dvec_ref[1] += fold(dbase)
            dstem = unit_back(dbase * param(0), hat, scale).astype(bf16)
            dws_ref[:, : pix.shape[0]] += dot(dstem, pix, ((1,), (1,)))

    @pl.when((phase == 2) & (slot == slots - 1))
    def _():
        mixed = dws_ref[...]
        for at in range(BLOCKS):
            mixed += lax.dot_general(
                dk_ref[:, at, :], pick_ref[at], (((1,), (0,)), ((), ())), precision=EXACT,
                preferred_element_type=f32,
            )
        products = dwr_ref[...]
        singles = [jnp.sum(dvec_ref[at], axis=1, keepdims=True) for at in range(3)]
        singles.append(jnp.sum(products * wr_ref[...].astype(f32), axis=1, keepdims=True))
        lane = lax.broadcasted_iota(jnp.int32, (channels, LANES), 1)
        start = first_single(pix_ref.shape[1])
        for at, single in enumerate(singles):
            mixed = jnp.where(lane == start + at, single, mixed)
        sums_ref[:channels] = mixed
        sums_ref[channels : channels + hidden] = dwe_ref[...]
        top = channels + hidden
        for at in range(hidden // LANES):
            sums_ref[top : top + channels] = products[:, at * LANES : (at + 1) * LANES] * par_ref[3]
            top += channels
        if top < sums_ref.shape[0]:
            sums_ref[top:] = jnp.zeros((sums_ref.shape[0] - top, LANES), f32)


def first_single(patch):
    return patch + KSIZE * KSIZE


def tap_places(patch):
    half = KSIZE // 2
    taps = KSIZE * KSIZE
    place = np.zeros((BLOCKS, taps, LANES), np.float32)
    pick = np.zeros((BLOCKS, LANES, LANES), np.float32)
    for m in range(BLOCKS):
        for r in range(2):
            a = m - 2 * PAD - r
            if abs(a) > half:
                continue
            for b in range(-half, half + 1):
                tap = (a + half) * KSIZE + b + half
                place[m, tap, (r * SIDE - b) % LANES] = 1.0
                k, rr = divmod(m, 2)
                pick[r * 5 + k, (rr * SIDE + b + SIDE - 1) % LANES, patch + tap] = 1.0
    return place, pick


def encode_slots(pixels, feature_grad, count, weights, share=1):
    (ws, stem_gain, stem_shift, kernel, block_gain, we, bias, wr, layer_scale) = weights
    slots, patch, area = pixels.shape
    channels = ws.shape[0]
    hidden = we.shape[0]
    pairs = area // LANES
    place, pick = tap_places(patch)
    total = channels + hidden + channels * (hidden // LANES)
    total = -(-total // (8 * share)) * 8 * share

    def pix_at(phase, slot, count):
        last = count[0] - 1
        return (jnp.where(phase == 1, last, jnp.minimum(slot, last)), 0, 0)

    def grad_at(phase, slot, count):
        return (jnp.where(phase == 0, 0, jnp.minimum(slot, count[0] - 1)), 0, 0)

    def feat_at(phase, slot, count):
        return (jnp.where(phase == 0, 0, jnp.where(phase == 1, slot, slots - 1)), 0, 0)

    def whole(shape):
        return pl.BlockSpec(shape, lambda phase, slot, count: (0,) * len(shape))

    consts = (
        ws, stem_gain[None], stem_shift[None], block_gain[None], layer_scale[None], kernel, we,
        bias[None], wr, jnp.asarray(place, bf16), jnp.asarray(place[:, ::-1], bf16),
        jnp.asarray(pick),
    )
    return pl.pallas_call(
        body,
        grid_spec=pltpu.PrefetchScalarGridSpec(
            num_scalar_prefetch=1,
            grid=(3, slots),
            in_specs=[
                pl.BlockSpec((1, patch, area), pix_at),
                pl.BlockSpec((1, channels, area), grad_at),
            ]
            + [whole(item.shape) for item in consts],
            out_specs=[pl.BlockSpec((1, channels, area), feat_at), whole((total, LANES))],
            scratch_shapes=[
                pltpu.VMEM((pairs + 2 * PAD, channels * slots, LANES), f32),
                pltpu.VMEM((pairs + 2 * PAD, channels * slots, LANES), f32),
                pltpu.VMEM((hidden, CHUNK), f32),
                pltpu.VMEM((hidden, CHUNK), f32),
                pltpu.VMEM((hidden, CHUNK), bf16),
                pltpu.VMEM((hidden, CHUNK), bf16),
                pltpu.VMEM((4, channels, LANES), f32),
                pltpu.VMEM((hidden, LANES), bf16),
                pltpu.VMEM((channels, hidden), bf16),
                pltpu.VMEM((hidden, channels), bf16),
                pltpu.VMEM((channels, 16, LANES), f32),
                pltpu.VMEM((channels, 16, LANES), f32),
                pltpu.VMEM((channels, LANES), f32),
                pltpu.VMEM((3, channels, LANES), f32),
                pltpu.VMEM((hidden, LANES), f32),
                pltpu.VMEM((channels, hidden), f32),
                pltpu.VMEM((channels, 16, LANES), f32),
            ],
        ),
        out_shape=[
            jax.ShapeDtypeStruct((slots, channels, area), bf16),
            jax.ShapeDtypeStruct((total, LANES), f32),
        ],
        compiler_params=pltpu.CompilerParams(
            dimension_semantics=("arbitrary", "arbitrary"), vmem_limit_bytes=60 * 2**20
        ),
    )(count, pixels, feature_grad, *consts)


def add_up(
    sums_ref, stem_ref, gain_ref, shift_ref, kernel_ref, norm_ref, expand_ref, bias_ref, reduce_ref,
    scale_ref, land_e, land_r, part, middle, full, out_sems, in_sems,
):
    count_e = lax.axis_size("enc")
    count_r = lax.axis_size("region")
    me_e = lax.axis_index("enc")
    me_r = lax.axis_index("region")
    barrier = pltpu.get_barrier_semaphore()
    for d in range(1, count_e):
        pl.semaphore_signal(
            barrier, 1, device_id={"enc": lax.rem(me_e + d, count_e)}, device_id_type=MESH
        )
    for d in range(1, count_r):
        pl.semaphore_signal(
            barrier, 1, device_id={"region": lax.rem(me_r + d, count_r)}, device_id_type=MESH
        )
    pl.semaphore_wait(barrier, count_e + count_r - 2)
    size_e = part.shape[0]
    size_r = land_r.shape[1]
    sems = iter(range(2 * (count_e + count_r - 2)))

    def block(index, size):
        return pl.ds(pl.multiple_of(index * size, 8), size)

    def exchange(axis, count, me, source, target):
        copies = []
        for d in range(1, count):
            peer = lax.rem(me + d, count)
            sem = next(sems)
            copy = pltpu.make_async_remote_copy(
                src_ref=source(peer), dst_ref=target(d), send_sem=out_sems.at[sem],
                recv_sem=in_sems.at[sem], device_id={axis: peer}, device_id_type=MESH,
            )
            copy.start()
            copies.append(copy)
        for copy in copies:
            copy.wait()

    exchange(
        "enc", count_e, me_e, lambda peer: sums_ref.at[block(peer, size_e)],
        lambda d: land_e.at[d - 1],
    )
    value = sums_ref[block(me_e, size_e)]
    for d in range(1, count_e):
        value += land_e[d - 1]
    part[...] = value
    exchange(
        "region", count_r, me_r, lambda peer: part.at[block(peer, size_r)],
        lambda d: land_r.at[d - 1],
    )
    value = part[block(me_r, size_r)]
    for d in range(1, count_r):
        value += land_r[d - 1]
    middle[block(me_r, size_r)] = value
    mine = middle.at[block(me_r, size_r)]
    exchange("region", count_r, me_r, lambda peer: mine, lambda d: mine)
    full[block(me_e, size_e)] = middle[...]
    own = full.at[block(me_e, size_e)]
    exchange("enc", count_e, me_e, lambda peer: own, lambda d: own)

    channels, patch = stem_ref.shape
    hidden = expand_ref.shape[0]
    mixed = full[:channels]
    stem_ref[...] = mixed[:, :patch]
    start = first_single(patch)
    kernel_ref[...] = mixed[:, patch:start]
    turned = jnp.transpose(mixed)
    for at, ref in enumerate((gain_ref, shift_ref, norm_ref, scale_ref)):
        ref[...] = turned[start + at : start + at + 1]
    wide_rows = full[channels : channels + hidden]
    expand_ref[...] = wide_rows[:, :channels]
    bias_ref[...] = jnp.transpose(wide_rows)[channels : channels + 1]
    top = channels + hidden
    for at in range(hidden // LANES):
        reduce_ref[:, at * LANES : (at + 1) * LANES] = full[top : top + channels]
        top += channels


def summed_over_devices(sums, weights):
    count_e = lax.axis_size("enc")
    count_r = lax.axis_size("region")
    size_e = sums.shape[0] // count_e
    size_r = size_e // count_r
    copies = 2 * (count_e + count_r - 2)
    shapes = [item.shape if item.ndim == 2 else (1, item.shape[0]) for item in weights]
    outs = pl.pallas_call(
        add_up,
        in_specs=[pl.BlockSpec(memory_space=pltpu.VMEM)],
        out_specs=[pl.BlockSpec(memory_space=pltpu.VMEM)] * len(shapes),
        out_shape=[jax.ShapeDtypeStruct(shape, f32) for shape in shapes],
        scratch_shapes=[
            pltpu.VMEM((count_e - 1, size_e, LANES), f32),
            pltpu.VMEM((count_r - 1, size_r, LANES), f32),
            pltpu.VMEM((size_e, LANES), f32),
            pltpu.VMEM((size_e, LANES), f32),
            pltpu.VMEM(sums.shape, f32),
            pltpu.SemaphoreType.DMA((copies,)),
            pltpu.SemaphoreType.DMA((copies,)),
        ],
        compiler_params=pltpu.CompilerParams(collective_id=0, has_side_effects=True),
    )(sums)
    return tuple(out.reshape(item.shape) for out, item in zip(outs, weights))


def on_device(pixels, feature_grad, tissue_count, *weights):
    share = lax.axis_size("enc") * lax.axis_size("region")
    features, sums = encode_slots(pixels, feature_grad, tissue_count, weights, share)
    return (features, *summed_over_devices(sums, weights))


def solution(mesh):
    return jax.shard_map(
        on_device,
        mesh=mesh,
        in_specs=(
            P(("region", "enc"), None, None),
            P(("region", "enc"), None, None),
            P(("region", "enc")),
        )
        + (P(),) * 9,
        out_specs=(P(("region", "enc"), None, None),) + (P(),) * 9,
        check_vma=False,
    )
```

profile of v0, /device:TPU:0, one launch (start us, length us, event | category | flops | bytes accessed | tf_op | source)
XLA Modules:
  0.0 210.4 jit_solution(9100883943625295251)
XLA Ops:
  1.3 1.2 broadcast_in_dim.19.bias_ref
  2.5 1.4 copy.25.ws_ref
  3.9 1.5 copy.26.kernel_ref
  5.4 1.6 copy.27.we_in_ref
  7.0 141.4 %shard_map.222 = (bf16[8,96,4096]{2,1,0:T(8,128)(2,1)}, f32[768,128]{1,0:T(8,128)}) custom-call(s32[1]{0:T(128)S(6)} %copy.36.count_ref, bf16[8,48,4096]{2,1,0:T(8,128)(2,1)} %pix_ref.1, bf16[8,96,4096]{2,1,0:T(8,128)(2,1)} %grad_ref.1, bf16[96,48]{1,0:T(8,128)(2,1)} %copy.25.ws_ref, f32[1,96]{1,0:T(1,128)} %bitcast.8, f32[1,96]{1,0:T(1,128)} %bitcast.9, ...), custom_call_target="tpu_custom_call" | custom-call | tf_op jit(solution)/shard_map/pallas_call | solution.py:323
  148.5 49.8 %shard_map.223 = (f32[96,48]{1,0:T(8,128)}, f32[1,96]{1,0:T(1,128)}, f32[1,96]{1,0:T(1,128)}, f32[96,49]{1,0:T(8,128)}, f32[1,96]{1,0:T(1,128)}, /*index=5*/f32[...) custom-call(f32[768,128]{1,0:T(8,128)} %get-tuple-element.22.sums_ref), custom_call_target="tpu_custom_call" | custom-call | tf_op jit(solution)/shard_map/pallas_call | solution.py:450
  198.3 1.5 copy.28
  199.8 1.3 reduce
  201.1 1.5 copy.29
  202.5 1.7 copy.30
  204.3 1.1 copy.37
  205.4 1.2 copy.38
  206.6 1.1 copy.39
  207.7 1.6 copy.40
  209.2 1.2 copy.41
where the time goes:
time: 211 us; the launch traced here: 210 us
  Pallas kernels  191 us (91%)
  local copies, waits for them, and re-layouts  16.6 us (8%)
    pallas_call x1, Pallas kernels, encode_slots(): pl.pallas_call(body, grid_spec=pltpu.PrefetchScalarGridSpec(num_scalar_pr...  141 us
    pallas_call x1, Pallas kernels, summed_over_devices(): pl.pallas_call(add_up, in_specs=[pl.BlockSpec(memory_space=pltpu.VMEM)],...  49.8 us
    unnamed x11, local copies, waits for them, and re-layouts  15.3 us

commit v1 on v0

v1 whole, which is shorter than its diff:
```python
import jax
import jax.numpy as jnp
import numpy as np
from jax import lax
from jax.experimental import pallas as pl
from jax.experimental.pallas import tpu as pltpu
from jax.sharding import PartitionSpec as P

SIDE = 64
KSIZE = 7
EPS = 1e-06
LANES = 128
CHUNK = 512
PAD = 2
BLOCKS = 8
HALF_PEAK = -0.3257480647361595
EXACT = lax.Precision.HIGHEST
MESH = pl.DeviceIdType.MESH

f32 = jnp.float32
bf16 = jnp.bfloat16


def dot(a, b, dims=((1,), (0,))):
    return lax.dot_general(a, b, (dims, ((), ())), preferred_element_type=f32)


def wide(value, times):
    return jnp.concatenate([value] * times, axis=1)


def fold(value):
    total = value[:, :LANES]
    for at in range(LANES, value.shape[1], LANES):
        total = total + value[:, at : at + LANES]
    return total


def unit(values):
    centre = jnp.mean(values, axis=0, keepdims=True)
    shifted = values - centre
    spread = jnp.mean(jnp.square(shifted), axis=0, keepdims=True)
    scale = lax.rsqrt(spread + EPS)
    return shifted * scale, scale


def gelu_twice(x):
    shape = 1.0 + lax.erf(x * 0.7071067811865476)
    decay = jnp.exp2(x * x * -0.7213475204444817 + HALF_PEAK)
    return x * shape, shape + x * decay


def body(
    count_ref, pix_hbm, grad_hbm, wst_ref, gain_ref, shift_ref, norm_ref, scale_ref, kernel_ref,
    wet_in_ref, bias_ref, wr_ref, place_ref, place_back_ref, pick_ref, feat_hbm, sums_ref, base_s,
    mix_s, pix_v, grad_v, feat_v, par_ref, ws_ref, we_ref, wet_ref, wrt_ref, wrs_ref, taps_ref,
    back_ref, dws_ref, dvec_ref, dwe_ref, dwr_ref, dk_ref, pix_sem, grad_sem, feat_sem,
):
    slots, channels, area = grad_v.shape
    patch = pix_v.shape[1]
    count = count_ref[0]
    pairs = area // LANES
    per = CHUNK // LANES
    chunks = area // CHUNK
    hidden = we_ref.shape[0]
    rows = slots

    def pix_copy(slot):
        return pltpu.make_async_copy(pix_hbm.at[slot], pix_v.at[slot], pix_sem.at[slot])

    def grad_copy(slot):
        return pltpu.make_async_copy(grad_hbm.at[slot], grad_v.at[slot], grad_sem.at[slot])

    def feat_copy(slot, side):
        return pltpu.make_async_copy(feat_v.at[side], feat_hbm.at[slot], feat_sem.at[side])

    @pl.loop(0, count)
    def _(slot):
        pix_copy(slot).start()

    @pl.loop(0, count)
    def _(slot):
        grad_copy(slot).start()

    row_at = lax.broadcasted_iota(jnp.int32, (SIDE, LANES), 0)
    lane_at = lax.broadcasted_iota(jnp.int32, (SIDE, LANES), 1) % SIDE
    near = jnp.abs(row_at - lane_at) <= KSIZE // 2
    row_all = lax.broadcasted_iota(jnp.int32, (LANES, LANES), 0)
    lane_all = lax.broadcasted_iota(jnp.int32, (LANES, LANES), 1)
    same = row_all // SIDE == lane_all // SIDE
    mirror = (same & (row_all % SIDE + lane_all % SIDE == SIDE - 1)).astype(f32).astype(bf16)

    def read(ref, slot, chunk):
        return jnp.concatenate(
            [
                ref[PAD + chunk * per + at, pl.ds(slot, channels, stride=rows), :]
                for at in range(per)
            ],
            axis=1,
        )

    def write(ref, slot, chunk, value):
        for at in range(per):
            ref[PAD + chunk * per + at, pl.ds(slot, channels, stride=rows), :] = value[
                :, at * LANES : (at + 1) * LANES
            ]

    def param(at):
        return wide(par_ref[at], per)

    def toeplitz(ref, c):
        blocks = []
        for m in range(BLOCKS):
            row = jnp.broadcast_to(ref[m, pl.ds(c, 1), :], (SIDE, LANES))
            turned = pltpu.roll(row, 0, 1, stride=1, stride_axis=0)
            blocks.append(jnp.where(near, turned, 0.0).astype(bf16))
        return jnp.concatenate(blocks, axis=0)

    lane_rows = lax.broadcasted_iota(jnp.int32, (pairs * rows, LANES), 1)

    def gathered(ref, c):
        at = pl.multiple_of(c * rows, rows)
        full = ref[:, pl.ds(at, rows), :]
        even = full.reshape((pairs + 2 * PAD) * rows, LANES).astype(bf16)
        odd = full[1 : pairs + 3].reshape((pairs + 2) * rows, LANES).astype(bf16)
        size = pairs * rows
        ends = jnp.where(lane_rows < SIDE, even[4 * rows : 4 * rows + size], even[:size])
        return jnp.concatenate(
            [odd[:size], even[2 * rows : 2 * rows + size], odd[2 * rows : 2 * rows + size], ends],
            axis=1,
        )

    edge = jnp.zeros((PAD, channels * rows, LANES), f32)
    for ref in (base_s, mix_s):
        ref[:PAD] = edge
        ref[PAD + pairs :] = edge
    for ref in (dws_ref, dvec_ref, dwe_ref, dwr_ref):
        ref[...] = jnp.zeros(ref.shape, f32)
    for at, ref in enumerate((gain_ref, shift_ref, norm_ref, scale_ref)):
        par_ref[at] = jnp.transpose(jnp.broadcast_to(ref[...], (LANES, channels)))
    kernel = jnp.transpose(kernel_ref[...]).astype(bf16)
    for m in range(BLOCKS):
        taps_ref[m] = dot(kernel, place_ref[m])
        back_ref[m] = dot(kernel, place_back_ref[m])
    stem = jnp.transpose(wst_ref[...].astype(f32))
    stem = stem - jnp.mean(stem, axis=0, keepdims=True)
    high = stem.astype(bf16)
    ws_ref[:, :patch] = high
    ws_ref[:, patch:] = (stem - high.astype(f32)).astype(bf16)
    weight = wet_in_ref[...].astype(f32) * wide(par_ref[2], hidden // LANES)
    weight = weight - jnp.mean(weight, axis=0, keepdims=True)
    wet_ref[...] = weight.astype(bf16)
    weight = jnp.transpose(weight)
    scaled = wr_ref[...].astype(f32) * (0.5 * wide(par_ref[3], hidden // LANES))
    wrs_ref[...] = scaled.astype(bf16)
    wrt_ref[...] = jnp.transpose(scaled).astype(bf16)
    bias = jnp.transpose(jnp.broadcast_to(bias_ref[...][None], (LANES, hidden)))
    high = bias.astype(bf16).astype(f32)
    middle = (bias - high).astype(bf16).astype(f32)
    low = bias - high - middle
    lane = lax.broadcasted_iota(jnp.int32, (hidden, LANES), 1)
    extra = jnp.where(
        lane == channels,
        high,
        jnp.where(lane == channels + 1, middle, jnp.where(lane == channels + 2, low, 0.0)),
    )
    we_ref[...] = extra.astype(bf16)
    we_ref[:, :channels] = weight.astype(bf16)

    def stem_hat(slot, at):
        pix = pix_v[slot, :, pl.ds(at, CHUNK)]
        out = dot(ws_ref[...], jnp.concatenate([pix, pix], axis=0))
        spread = jnp.mean(jnp.square(out), axis=0, keepdims=True)
        scale = lax.rsqrt(spread + EPS)
        return out * scale, scale, pix

    @pl.loop(0, count)
    def _(slot):
        pix_copy(slot).wait()

        @pl.loop(0, chunks, unroll=4)
        def _(chunk):
            at = pl.multiple_of(chunk * CHUNK, CHUNK)
            hat, _, _ = stem_hat(slot, at)
            write(base_s, slot, chunk, hat * param(0) + param(1))

    @pl.loop(count, slots)
    def _(slot):
        @pl.loop(0, chunks)
        def _(chunk):
            write(base_s, slot, chunk, jnp.zeros((channels, CHUNK), f32))

    @pl.loop(0, channels, unroll=8)
    def _(c):
        out = dot(gathered(base_s, c), toeplitz(taps_ref, c))
        at = pl.multiple_of(c * rows, rows)
        mix_s[PAD : PAD + pairs, pl.ds(at, rows), :] = out.reshape(pairs, rows, LANES)

    @pl.loop(0, count)
    def _(slot):
        side = slot % 2
        grad_copy(slot).wait()

        @pl.when(slot >= 2)
        def _():
            feat_copy(slot, side).wait()

        @pl.loop(0, chunks, unroll=4)
        def _(chunk):
            at = pl.multiple_of(chunk * CHUNK, CHUNK)
            hat, scale = unit(read(mix_s, slot, chunk))
            normed = jnp.concatenate(
                [hat.astype(bf16), jnp.ones((LANES - channels, CHUNK), bf16)], axis=0
            )
            grad = grad_v[slot, :, pl.ds(at, CHUNK)]
            ex = dot(we_ref[...], normed)
            dh = dot(wrt_ref[...], grad)
            acts, slopes = [], []
            for h in range(0, hidden, 16):
                act, slope = gelu_twice(ex[h : h + 16])
                acts.append(act.astype(bf16))
                slopes.append((slope * dh[h : h + 16]).astype(bf16))
            hid = jnp.concatenate(acts, axis=0)
            de = jnp.concatenate(slopes, axis=0)
            reduced = dot(wrs_ref[...], hid)
            feat_v[side, :, pl.ds(at, CHUNK)] = (read(base_s, slot, chunk) + reduced).astype(bf16)
            dwr_ref[...] += dot(grad, hid, ((1,), (1,)))
            dwe_ref[...] += dot(de, normed, ((1,), (1,)))
            dn = dot(wet_ref[...], de)
            second = jnp.mean(dn * hat, axis=0, keepdims=True)
            write(mix_s, slot, chunk, scale * (dn - hat * second))

        feat_copy(slot, side).start()

    @pl.loop(count, slots)
    def _(slot):
        side = slot % 2

        @pl.when(slot >= 2)
        def _():
            feat_copy(slot, side).wait()

        @pl.loop(0, chunks)
        def _(chunk):
            at = pl.multiple_of(chunk * CHUNK, CHUNK)
            feat_v[side, :, pl.ds(at, CHUNK)] = jnp.zeros((channels, CHUNK), bf16)

        feat_copy(slot, side).start()

    lane_one = lax.broadcasted_iota(jnp.int32, (8, LANES), 1)
    lane_half = lane_one % SIDE
    lower = (lane_one >= 3) & (lane_one < SIDE + 3)

    def banded(cross, r, k, turn):
        def tall(v):
            return cross[r * SIDE + 8 * v : r * SIDE + 8 * v + 8, k * LANES : (k + 1) * LANES]

        even = jnp.where(lane_half < 4, 0.0, tall(6))
        for v in (4, 2, 0):
            even = jnp.where(lane_half >= 52 - 8 * v, tall(v), even)
        odd = tall(7)
        for v in (5, 3, 1):
            odd = jnp.where(lane_half >= 52 - 8 * v, tall(v), odd)
        odd = jnp.where(lane_half >= 60, 0.0, odd)
        return pltpu.roll(even, turn, 1, stride=1, stride_axis=0) + pltpu.roll(
            odd, turn + 8, 1, stride=1, stride_axis=0
        )

    @pl.loop(0, channels, unroll=8)
    def _(c):
        at = pl.multiple_of(c * rows, rows)
        grad = mix_s[PAD : PAD + pairs, pl.ds(at, rows), :]
        grad = grad.reshape(pairs * rows, LANES).astype(bf16)
        grad = dot(mirror, grad, ((1,), (1,))).astype(bf16)
        cross = dot(grad, gathered(base_s, c))
        first = [banded(cross, 0, k, 0) for k in (3, 0, 1, 2)]
        second = [banded(cross, 1, k, SIDE) for k in (0, 1, 2, 3)]
        taken = [second[0]] + [
            jnp.where(lower, second[k - 1], second[k]) for k in range(1, 4)
        ]
        for k in range(4):
            dk_ref[k, pl.ds(c, 1), :] = jnp.sum(first[k] + taken[k], axis=0, keepdims=True)
        out = dot(gathered(mix_s, c), toeplitz(back_ref, c))
        mix_s[PAD : PAD + pairs, pl.ds(at, rows), :] = out.reshape(pairs, rows, LANES)

    @pl.loop(0, count)
    def _(slot):
        @pl.loop(0, chunks, unroll=4)
        def _(chunk):
            at = pl.multiple_of(chunk * CHUNK, CHUNK)
            hat, scale, pix = stem_hat(slot, at)
            dbase = grad_v[slot, :, pl.ds(at, CHUNK)].astype(f32) + read(mix_s, slot, chunk)
            turned = dbase * hat
            dvec_ref[0] += fold(turned)
            dvec_ref[1] += fold(dbase)
            scaled = dbase * param(0)
            first = jnp.mean(scaled, axis=0, keepdims=True)
            second = jnp.mean(turned * param(0), axis=0, keepdims=True)
            dstem = (scale * (scaled - first - hat * second)).astype(bf16)
            dws_ref[:, :patch] += dot(dstem, pix, ((1,), (1,)))

    mixed = dws_ref[...]
    for at in range(4):
        mixed += lax.dot_general(
            dk_ref[at], pick_ref[at], (((1,), (0,)), ((), ())), precision=EXACT,
            preferred_element_type=f32,
        )
    products = dwr_ref[...] * 0.5
    expand = jnp.transpose(dwe_ref[...])
    singles = [jnp.sum(dvec_ref[at], axis=1, keepdims=True) for at in range(2)]
    singles.append(
        jnp.sum(expand[:channels] * wet_in_ref[...].astype(f32), axis=1, keepdims=True)
    )
    singles.append(jnp.sum(products * wr_ref[...].astype(f32), axis=1, keepdims=True))
    lane = lax.broadcasted_iota(jnp.int32, (channels, LANES), 1)
    start = first_single(patch)
    for at, single in enumerate(singles):
        mixed = jnp.where(lane == start + at, single, mixed)
    mixed = jnp.concatenate([mixed, jnp.zeros((LANES - channels, LANES), f32)], axis=0)
    top = first_bias(patch)
    sums_ref[:top] = jnp.transpose(mixed)[:top]
    products = products * wide(par_ref[3], hidden // LANES)
    tail = expand[channels : channels + 1]
    expand = expand[:channels] * wide(par_ref[2], hidden // LANES)
    for at in range(hidden // LANES):
        sums_ref[top : top + 1] = tail[:, at * LANES : (at + 1) * LANES]
        top += 1
    for value in (expand, products):
        for at in range(hidden // LANES):
            sums_ref[top : top + channels] = value[:, at * LANES : (at + 1) * LANES]
            top += channels
    if top < sums_ref.shape[0]:
        sums_ref[top:] = jnp.zeros((sums_ref.shape[0] - top, LANES), f32)
    for side in range(min(2, slots)):
        feat_copy(side, side).wait()


def first_single(patch):
    return patch + KSIZE * KSIZE


def first_bias(patch):
    return first_single(patch) + 4


def total_rows(patch, channels, hidden, share):
    blocks = hidden // LANES
    total = first_bias(patch) + blocks + 2 * channels * blocks
    return -(-total // share) * share


def tap_places(patch):
    half = KSIZE // 2
    taps = KSIZE * KSIZE
    place = np.zeros((BLOCKS, taps, LANES), np.float32)
    for at, m in enumerate((2, 3, 4, 5, 6, 7, 8, 1)):
        for r in range(2):
            a = m - 2 * PAD - r
            if abs(a) > half:
                continue
            for b in range(-half, half + 1):
                place[at, (a + half) * KSIZE + b + half, (r * SIDE - b) % LANES] = 1.0
    pick = np.zeros((4, LANES, LANES), np.float32)
    for k in range(4):
        for rr in range(2):
            a = 2 * (k - PAD) + rr
            if abs(a) > half:
                continue
            for b in range(-half, half + 1):
                for step in range(4):
                    lane = (rr * SIDE + SIDE - 1 - 16 * step + b) % LANES
                    pick[k, lane, patch + (a + half) * KSIZE + b + half] = 1.0
    return place, pick


def encode_slots(pixels, feature_grad, count, weights, share=1):
    (ws, stem_gain, stem_shift, kernel, block_gain, we, bias, wr, layer_scale) = weights
    slots, patch, area = pixels.shape
    channels = ws.shape[0]
    hidden = we.shape[0]
    pairs = area // LANES
    place, pick = tap_places(patch)
    total = total_rows(patch, channels, hidden, share)
    consts = (
        ws.T, stem_gain[None], stem_shift[None], block_gain[None], layer_scale[None], kernel.T,
        we.T, bias, wr, jnp.asarray(place, bf16),
        jnp.asarray(place[:, ::-1], bf16), jnp.asarray(pick),
    )
    vmem = pl.BlockSpec(memory_space=pltpu.VMEM)
    hbm = pl.BlockSpec(memory_space=pl.ANY)
    return pl.pallas_call(
        body,
        in_specs=[pl.BlockSpec(memory_space=pltpu.SMEM), hbm, hbm] + [vmem] * len(consts),
        out_specs=[hbm, vmem],
        scratch_shapes=[
            pltpu.VMEM((pairs + 2 * PAD, channels * slots, LANES), f32),
            pltpu.VMEM((pairs + 2 * PAD, channels * slots, LANES), f32),
            pltpu.VMEM((slots, patch, area), bf16),
            pltpu.VMEM((slots, channels, area), bf16),
            pltpu.VMEM((2, channels, area), bf16),
            pltpu.VMEM((4, channels, LANES), f32),
            pltpu.VMEM((channels, 2 * patch), bf16),
            pltpu.VMEM((hidden, LANES), bf16),
            pltpu.VMEM((channels, hidden), bf16),
            pltpu.VMEM((hidden, channels), bf16),
            pltpu.VMEM((channels, hidden), bf16),
            pltpu.VMEM((BLOCKS, channels, LANES), f32),
            pltpu.VMEM((BLOCKS, channels, LANES), f32),
            pltpu.VMEM((channels, LANES), f32),
            pltpu.VMEM((2, channels, LANES), f32),
            pltpu.VMEM((hidden, LANES), f32),
            pltpu.VMEM((channels, hidden), f32),
            pltpu.VMEM((4, channels, LANES), f32),
            pltpu.SemaphoreType.DMA((slots,)),
            pltpu.SemaphoreType.DMA((slots,)),
            pltpu.SemaphoreType.DMA((2,)),
        ],
        out_shape=[
            jax.ShapeDtypeStruct((slots, channels, area), bf16),
            jax.ShapeDtypeStruct((total, LANES), f32),
        ],
        compiler_params=pltpu.CompilerParams(vmem_limit_bytes=60 * 2**20),
    )(count, pixels, feature_grad, *consts)


def add_up(sums_ref, out_ref, outgoing, land_e, land_r, full, out_sems, in_sems):
    count_e = lax.axis_size("enc")
    count_r = lax.axis_size("region")
    me_e = lax.axis_index("enc")
    me_r = lax.axis_index("region")
    barrier = pltpu.get_barrier_semaphore()
    for d in range(1, count_e):
        pl.semaphore_signal(
            barrier, 1, device_id={"enc": lax.rem(me_e + d, count_e)}, device_id_type=MESH
        )
    for d in range(1, count_r):
        pl.semaphore_signal(
            barrier, 1, device_id={"region": lax.rem(me_r + d, count_r)}, device_id_type=MESH
        )
    outgoing[...] = sums_ref[...].astype(bf16)
    pl.semaphore_wait(barrier, count_e + count_r - 2)
    size = land_e.shape[1]
    sems = iter(range(2 * (count_e - 1) + count_r - 1))

    def block(index):
        return pl.ds(pl.multiple_of(index * size, 16), size)

    def exchange(axis, count, me, source, target):
        copies = []
        for d in range(1, count):
            peer = lax.rem(me + d, count)
            sem = next(sems)
            copy = pltpu.make_async_remote_copy(
                src_ref=source(peer), dst_ref=target(d), send_sem=out_sems.at[sem],
                recv_sem=in_sems.at[sem], device_id={axis: peer}, device_id_type=MESH,
            )
            copy.start()
            copies.append(copy)
        for copy in copies:
            copy.wait()

    exchange(
        "enc", count_e, me_e, lambda peer: outgoing.at[block(peer)], lambda d: land_e.at[d - 1]
    )
    value = sums_ref[block(me_e)]
    for d in range(1, count_e):
        value += land_e[d - 1].astype(f32)
    land_r[me_r] = value.astype(bf16)
    mine = land_r.at[me_r]
    exchange("region", count_r, me_r, lambda peer: mine, lambda d: mine)
    value = land_r[0].astype(f32)
    for at in range(1, count_r):
        value += land_r[at].astype(f32)
    full[block(me_e)] = value.astype(bf16)
    own = full.at[block(me_e)]
    exchange("enc", count_e, me_e, lambda peer: own, lambda d: own)
    out_ref[...] = full[...]


def unpack(
    full_ref, stem_ref, gain_ref, shift_ref, kernel_ref, norm_ref, expand_ref, bias_ref, reduce_ref,
    scale_ref,
):
    patch, channels = stem_ref.shape
    hidden = expand_ref.shape[1]
    full = full_ref[...].astype(f32)
    start = first_single(patch)
    stem_ref[...] = full[:patch, :channels]
    kernel_ref[...] = full[patch:start, :channels]
    for at, ref in enumerate((gain_ref, shift_ref, norm_ref, scale_ref)):
        ref[...] = full[start + at : start + at + 1, :channels]
    top = first_bias(patch)
    parts = range(hidden // LANES)
    for at in parts:
        bias_ref[at * LANES : (at + 1) * LANES] = full[top + at]
    top += len(parts)
    for ref in (expand_ref, reduce_ref):
        for at in parts:
            ref[:, at * LANES : (at + 1) * LANES] = full[top : top + channels]
            top += channels


def summed_over_devices(sums, weights):
    (ws, stem_gain, stem_shift, kernel, block_gain, we, bias, wr, layer_scale) = weights
    count_e = lax.axis_size("enc")
    count_r = lax.axis_size("region")
    size = sums.shape[0] // count_e
    copies = 2 * (count_e - 1) + count_r - 1
    vmem = pl.BlockSpec(memory_space=pltpu.VMEM)
    full = pl.pallas_call(
        add_up,
        in_specs=[vmem],
        out_specs=vmem,
        out_shape=jax.ShapeDtypeStruct(sums.shape, bf16),
        scratch_shapes=[
            pltpu.VMEM(sums.shape, bf16),
            pltpu.VMEM((count_e - 1, size, LANES), bf16),
            pltpu.VMEM((count_r, size, LANES), bf16),
            pltpu.VMEM(sums.shape, bf16),
            pltpu.SemaphoreType.DMA((copies,)),
            pltpu.SemaphoreType.DMA((copies,)),
        ],
        compiler_params=pltpu.CompilerParams(collective_id=0, has_side_effects=True),
    )(sums)
    shapes = [
        ws.shape[::-1], (1, stem_gain.shape[0]), (1, stem_shift.shape[0]), kernel.shape[::-1],
        (1, block_gain.shape[0]), we.shape[::-1], bias.shape, wr.shape, (1, layer_scale.shape[0]),
    ]
    outs = pl.pallas_call(
        unpack,
        in_specs=[vmem],
        out_specs=[vmem] * len(shapes),
        out_shape=[jax.ShapeDtypeStruct(shape, f32) for shape in shapes],
    )(full)
    stem, gain, shift, kernel, norm, expand, bias, reduce, scale = outs
    return (
        stem.T, gain[0], shift[0], kernel.T, norm[0], expand.T, bias, reduce, scale[0],
    )


def on_device(pixels, feature_grad, tissue_count, *weights):
    share = 16 * lax.axis_size("enc")
    features, sums = encode_slots(pixels, feature_grad, tissue_count, weights, share)
    return (features, *summed_over_devices(sums, weights))


def solution(mesh):
    return jax.shard_map(
        on_device,
        mesh=mesh,
        in_specs=(
            P(("region", "enc"), None, None),
            P(("region", "enc"), None, None),
            P(("region", "enc")),
        )
        + (P(),) * 9,
        out_specs=(P(("region", "enc"), None, None),) + (P(),) * 9,
        check_vma=False,
    )
```

time: 211 us -> 142 us (0.67)
  Pallas kernels: 191 us -> 141 us
  local copies, waits for them, and re-layouts: 16.6 us -> 0 us
    pallas_call x2 -> x3, Pallas kernels: 191 us -> 141 us  [the longest x1 84.9 us: summed_over_devices(): pl.pallas_call(add_up, in_specs=[vmem], out_specs=vmem, out_shape=jax.Sha...]
    unnamed x11 -> x0, local copies, waits for them, and re-layouts: 15.3 us -> none
where the time goes in v1:
time: 142 us
  Pallas kernels  141 us (99%)
    pallas_call x1, Pallas kernels, summed_over_devices(): pl.pallas_call(add_up, in_specs=[vmem], out_specs=vmem, out_shape=jax.Sha...  84.9 us
    pallas_call x1, Pallas kernels, encode_slots(): pl.pallas_call(body, in_specs=[pl.BlockSpec(memory_space=pltpu.SMEM), hbm...  54 us

profile of v1, /device:TPU:0, one launch (start us, length us, event | category | flops | bytes accessed | tf_op | source)
XLA Modules:
  0.0 142.0 jit_solution(3049331581853630906)
XLA Ops:
  1.3 54.0 %shard_map.222 = (bf16[8,96,4096]{2,1,0:T(8,128)(2,1)}, f32[768,128]{1,0:T(8,128)}) custom-call(s32[1]{0:T(128)S(6)} %copy.25.count_ref, bf16[8,48,4096]{2,1,0:T(8,128)(2,1)} %pix_hbm.1, bf16[8,96,4096]{2,1,0:T(8,128)(2,1)} %grad_hbm.1, bf16[48,96]{1,0:T(8,128)(2,1)} %bitcast.16, f32[1,96]{1,0:T(1,128)} %bitcast.17, f32[1,96]{1,0:T(1,128)} %bitcast.18, ...), custom_call_target="tpu_custom_call" | custom-call | tf_op jit(solution)/shard_map/pallas_call | solution.py:391
  55.3 84.9 %shard_map.223.full_ref = bf16[768,128]{1,0:T(8,128)(2,1)} custom-call(f32[768,128]{1,0:T(8,128)} %get-tuple-element.22.sums_ref), custom_call_target="tpu_custom_call" | custom-call | tf_op jit(solution)/shard_map/pallas_call | solution.py:510
  140.3 1.7 %shard_map.224 = (f32[48,96]{1,0:T(8,128)}, f32[1,96]{1,0:T(1,128)}, f32[1,96]{1,0:T(1,128)}, f32[49,96]{1,0:T(8,128)}, f32[1,96]{1,0:T(1,128)}, /*index=5*/f32[...) custom-call(bf16[768,128]{1,0:T(8,128)(2,1)} %shard_map.223.full_ref), custom_call_target="tpu_custom_call" | custom-call | tf_op jit(solution)/shard_map/pallas_call | solution.py:529

commit v2 on v1

--- a/solution.py
+++ b/solution.py
@@ -46,8 +46,10 @@
 
 def gelu_twice(x):
     shape = 1.0 + lax.erf(x * 0.7071067811865476)
-    decay = jnp.exp2(x * x * -0.7213475204444817 + HALF_PEAK)
-    return x * shape, shape + x * decay
+    act = (x * shape).astype(bf16)
+    x = x.astype(bf16)
+    decay = jnp.exp2(x * x * bf16(-0.7213475204444817) + bf16(HALF_PEAK))
+    return act, shape.astype(bf16) + x * decay
 
 
 def body(
@@ -74,13 +76,7 @@
     def feat_copy(slot, side):
         return pltpu.make_async_copy(feat_v.at[side], feat_hbm.at[slot], feat_sem.at[side])
 
-    @pl.loop(0, count)
-    def _(slot):
-        pix_copy(slot).start()
-
-    @pl.loop(0, count)
-    def _(slot):
-        grad_copy(slot).start()
+    pix_copy(0).start()
 
     row_at = lax.broadcasted_iota(jnp.int32, (SIDE, LANES), 0)
     lane_at = lax.broadcasted_iota(jnp.int32, (SIDE, LANES), 1) % SIDE
@@ -178,6 +174,12 @@
     def _(slot):
         pix_copy(slot).wait()
 
+        @pl.when(slot + 1 < count)
+        def _():
+            pix_copy(slot + 1).start()
+
+        grad_copy(slot).start()
+
         @pl.loop(0, chunks, unroll=4)
         def _(chunk):
             at = pl.multiple_of(chunk * CHUNK, CHUNK)
@@ -190,7 +192,7 @@
         def _(chunk):
             write(base_s, slot, chunk, jnp.zeros((channels, CHUNK), f32))
 
-    @pl.loop(0, channels, unroll=8)
+    @pl.loop(0, channels, unroll=16)
     def _(c):
         out = dot(gathered(base_s, c), toeplitz(taps_ref, c))
         at = pl.multiple_of(c * rows, rows)
@@ -205,7 +207,7 @@
         def _():
             feat_copy(slot, side).wait()
 
-        @pl.loop(0, chunks, unroll=4)
+        @pl.loop(0, chunks, unroll=8)
         def _(chunk):
             at = pl.multiple_of(chunk * CHUNK, CHUNK)
             hat, scale = unit(read(mix_s, slot, chunk))
@@ -214,17 +216,17 @@
             )
             grad = grad_v[slot, :, pl.ds(at, CHUNK)]
             ex = dot(we_ref[...], normed)
-            dh = dot(wrt_ref[...], grad)
+            dh = dot(wrt_ref[...], grad).astype(bf16)
             acts, slopes = [], []
             for h in range(0, hidden, 16):
                 act, slope = gelu_twice(ex[h : h + 16])
-                acts.append(act.astype(bf16))
-                slopes.append((slope * dh[h : h + 16]).astype(bf16))
+                acts.append(act)
+                slopes.append(slope * dh[h : h + 16])
             hid = jnp.concatenate(acts, axis=0)
             de = jnp.concatenate(slopes, axis=0)
             reduced = dot(wrs_ref[...], hid)
             feat_v[side, :, pl.ds(at, CHUNK)] = (read(base_s, slot, chunk) + reduced).astype(bf16)
-            dwr_ref[...] += dot(grad, hid, ((1,), (1,)))
+            dwr_ref[:, :channels] += dot(hid, grad, ((1,), (1,)))
             dwe_ref[...] += dot(de, normed, ((1,), (1,)))
             dn = dot(wet_ref[...], de)
             second = jnp.mean(dn * hat, axis=0, keepdims=True)
@@ -290,24 +292,27 @@
             at = pl.multiple_of(chunk * CHUNK, CHUNK)
             hat, scale, pix = stem_hat(slot, at)
             dbase = grad_v[slot, :, pl.ds(at, CHUNK)].astype(f32) + read(mix_s, slot, chunk)
-            turned = dbase * hat
-            dvec_ref[0] += fold(turned)
-            dvec_ref[1] += fold(dbase)
-            scaled = dbase * param(0)
-            first = jnp.mean(scaled, axis=0, keepdims=True)
-            second = jnp.mean(turned * param(0), axis=0, keepdims=True)
-            dstem = (scale * (scaled - first - hat * second)).astype(bf16)
-            dws_ref[:, :patch] += dot(dstem, pix, ((1,), (1,)))
-
-    mixed = dws_ref[...]
+            dvec_ref[...] += fold(dbase)
+            second = jnp.mean(dbase * hat * param(0), axis=0, keepdims=True)
+            straight = (scale * dbase).astype(bf16)
+            along = (hat * (scale * second)).astype(bf16)
+            both = dot(jnp.concatenate([straight, along], axis=0), pix, ((1,), (1,)))
+            dws_ref[:, :, :patch] += both.reshape(2, channels, patch)
+
+    mixed = dws_ref[0] * par_ref[0] - dws_ref[1]
+    mixed = mixed - jnp.mean(mixed, axis=0, keepdims=True)
     for at in range(4):
         mixed += lax.dot_general(
             dk_ref[at], pick_ref[at], (((1,), (0,)), ((), ())), precision=EXACT,
             preferred_element_type=f32,
         )
-    products = dwr_ref[...] * 0.5
+    products = jnp.transpose(dwr_ref[...])[:channels] * 0.5
     expand = jnp.transpose(dwe_ref[...])
-    singles = [jnp.sum(dvec_ref[at], axis=1, keepdims=True) for at in range(2)]
+    stem = ws_ref[:, :patch].astype(f32) + ws_ref[:, patch:].astype(f32)
+    singles = [
+        jnp.sum(dws_ref[0, :, :patch] * stem, axis=1, keepdims=True),
+        jnp.sum(dvec_ref[...], axis=1, keepdims=True),
+    ]
     singles.append(
         jnp.sum(expand[:channels] * wet_in_ref[...].astype(f32), axis=1, keepdims=True)
     )
@@ -406,10 +411,10 @@
             pltpu.VMEM((channels, hidden), bf16),
             pltpu.VMEM((BLOCKS, channels, LANES), f32),
             pltpu.VMEM((BLOCKS, channels, LANES), f32),
+            pltpu.VMEM((2, channels, LANES), f32),
             pltpu.VMEM((channels, LANES), f32),
-            pltpu.VMEM((2, channels, LANES), f32),
             pltpu.VMEM((hidden, LANES), f32),
-            pltpu.VMEM((channels, hidden), f32),
+            pltpu.VMEM((hidden, LANES), f32),
             pltpu.VMEM((4, channels, LANES), f32),
             pltpu.SemaphoreType.DMA((slots,)),
             pltpu.SemaphoreType.DMA((slots,)),

time: 142 us -> 133 us (0.937)
  Pallas kernels: 141 us -> 131 us
    pallas_call x1, Pallas kernels: 84.9 us -> 43.9 us  [summed_over_devices(): pl.pallas_call(add_up, in_specs=[vmem], out_specs=vmem, out_shape=jax.Sha...]
    pallas_call x1, Pallas kernels: 54 us -> 85.2 us  [encode_slots(): pl.pallas_call(body, in_specs=[pl.BlockSpec(memory_space=pltpu.SMEM), hbm...]
where the time goes in v2:
time: 133 us; the launch traced here: 132 us
  Pallas kernels  131 us (98%)
    pallas_call x1, Pallas kernels, encode_slots(): pl.pallas_call(body, in_specs=[pl.BlockSpec(memory_space=pltpu.SMEM), hbm...  85.2 us
    pallas_call x1, Pallas kernels, summed_over_devices(): pl.pallas_call(add_up, in_specs=[vmem], out_specs=vmem, out_shape=jax.Sha...  43.9 us

profile of v2, /device:TPU:0, one launch (start us, length us, event | category | flops | bytes accessed | tf_op | source)
XLA Modules:
  0.0 132.1 jit_solution(1405931213704460128)
XLA Ops:
  1.3 85.2 %shard_map.222 = (bf16[8,96,4096]{2,1,0:T(8,128)(2,1)}, f32[768,128]{1,0:T(8,128)}) custom-call(s32[1]{0:T(128)S(6)} %copy.25.count_ref, bf16[8,48,4096]{2,1,0:T(8,128)(2,1)} %pix_hbm.1, bf16[8,96,4096]{2,1,0:T(8,128)(2,1)} %grad_hbm.1, bf16[48,96]{1,0:T(8,128)(2,1)} %bitcast.16, f32[1,96]{1,0:T(1,128)} %bitcast.17, f32[1,96]{1,0:T(1,128)} %bitcast.18, ...), custom_call_target="tpu_custom_call" | custom-call | tf_op jit(solution)/shard_map/pallas_call | solution.py:396
  86.5 43.9 %shard_map.223.full_ref = bf16[768,128]{1,0:T(8,128)(2,1)} custom-call(f32[768,128]{1,0:T(8,128)} %get-tuple-element.22.sums_ref), custom_call_target="tpu_custom_call" | custom-call | tf_op jit(solution)/shard_map/pallas_call | solution.py:515
  130.4 1.7 %shard_map.224 = (f32[48,96]{1,0:T(8,128)}, f32[1,96]{1,0:T(1,128)}, f32[1,96]{1,0:T(1,128)}, f32[49,96]{1,0:T(8,128)}, f32[1,96]{1,0:T(1,128)}, /*index=5*/f32[...) custom-call(bf16[768,128]{1,0:T(8,128)(2,1)} %shard_map.223.full_ref), custom_call_target="tpu_custom_call" | custom-call | tf_op jit(solution)/shard_map/pallas_call | solution.py:534

commit v3 on v2

--- a/solution.py
+++ b/solution.py
@@ -46,10 +46,10 @@
 
 def gelu_twice(x):
     shape = 1.0 + lax.erf(x * 0.7071067811865476)
-    act = (x * shape).astype(bf16)
+    shape = shape.astype(bf16)
     x = x.astype(bf16)
     decay = jnp.exp2(x * x * bf16(-0.7213475204444817) + bf16(HALF_PEAK))
-    return act, shape.astype(bf16) + x * decay
+    return x * shape, shape + x * decay
 
 
 def body(
@@ -180,7 +180,7 @@
 
         grad_copy(slot).start()
 
-        @pl.loop(0, chunks, unroll=4)
+        @pl.loop(0, chunks, unroll=8)
         def _(chunk):
             at = pl.multiple_of(chunk * CHUNK, CHUNK)
             hat, _, _ = stem_hat(slot, at)

time: 133 us -> 131 us (0.985)
    pallas_call x1, Pallas kernels: 43.9 us -> 35.1 us  [summed_over_devices(): pl.pallas_call(add_up, in_specs=[vmem], out_specs=vmem, out_shape=jax.Sha...]
    pallas_call x1, Pallas kernels: 85.2 us -> 92.7 us  [encode_slots(): pl.pallas_call(body, in_specs=[pl.BlockSpec(memory_space=pltpu.SMEM), hbm...]
where the time goes in v3:
time: 131 us
  Pallas kernels  130 us (99%)
  between operations  1.31 us (1%)
    pallas_call x1, Pallas kernels, encode_slots(): pl.pallas_call(body, in_specs=[pl.BlockSpec(memory_space=pltpu.SMEM), hbm...  92.7 us
    pallas_call x1, Pallas kernels, summed_over_devices(): pl.pallas_call(add_up, in_specs=[vmem], out_specs=vmem, out_shape=jax.Sha...  35.1 us

profile of v3, /device:TPU:0, one launch (start us, length us, event | category | flops | bytes accessed | tf_op | source)
XLA Modules:
  0.0 130.8 jit_solution(734866359561006692)
XLA Ops:
  1.3 92.7 %shard_map.222 = (bf16[8,96,4096]{2,1,0:T(8,128)(2,1)}, f32[768,128]{1,0:T(8,128)}) custom-call(s32[1]{0:T(128)S(6)} %copy.25.count_ref, bf16[8,48,4096]{2,1,0:T(8,128)(2,1)} %pix_hbm.1, bf16[8,96,4096]{2,1,0:T(8,128)(2,1)} %grad_hbm.1, bf16[48,96]{1,0:T(8,128)(2,1)} %bitcast.16, f32[1,96]{1,0:T(1,128)} %bitcast.17, f32[1,96]{1,0:T(1,128)} %bitcast.18, ...), custom_call_target="tpu_custom_call" | custom-call | tf_op jit(solution)/shard_map/pallas_call | solution.py:396
  94.0 35.1 %shard_map.223.full_ref = bf16[768,128]{1,0:T(8,128)(2,1)} custom-call(f32[768,128]{1,0:T(8,128)} %get-tuple-element.22.sums_ref), custom_call_target="tpu_custom_call" | custom-call | tf_op jit(solution)/shard_map/pallas_call | solution.py:515
  129.2 1.7 %shard_map.224 = (f32[48,96]{1,0:T(8,128)}, f32[1,96]{1,0:T(1,128)}, f32[1,96]{1,0:T(1,128)}, f32[49,96]{1,0:T(8,128)}, f32[1,96]{1,0:T(1,128)}, /*index=5*/f32[...) custom-call(bf16[768,128]{1,0:T(8,128)(2,1)} %shard_map.223.full_ref), custom_call_target="tpu_custom_call" | custom-call | tf_op jit(solution)/shard_map/pallas_call | solution.py:534

commit v4 on v3

--- a/solution.py
+++ b/solution.py
@@ -76,7 +76,9 @@
     def feat_copy(slot, side):
         return pltpu.make_async_copy(feat_v.at[side], feat_hbm.at[slot], feat_sem.at[side])
 
-    pix_copy(0).start()
+    @pl.loop(0, count)
+    def _(slot):
+        pix_copy(slot).start()
 
     row_at = lax.broadcasted_iota(jnp.int32, (SIDE, LANES), 0)
     lane_at = lax.broadcasted_iota(jnp.int32, (SIDE, LANES), 1) % SIDE
@@ -173,10 +175,6 @@
     @pl.loop(0, count)
     def _(slot):
         pix_copy(slot).wait()
-
-        @pl.when(slot + 1 < count)
-        def _():
-            pix_copy(slot + 1).start()
 
         grad_copy(slot).start()
 

time: 131 us -> 130 us (level)
  Pallas kernels: 130 us -> 128 us
    pallas_call x1, Pallas kernels: 92.7 us -> 51.2 us  [encode_slots(): pl.pallas_call(body, in_specs=[pl.BlockSpec(memory_space=pltpu.SMEM), hbm...]
    pallas_call x1, Pallas kernels: 35.1 us -> 75.3 us  [summed_over_devices(): pl.pallas_call(add_up, in_specs=[vmem], out_specs=vmem, out_shape=jax.Sha...]
where the time goes in v4:
time: 130 us; the launch traced here: 129 us
  Pallas kernels  128 us (98%)
  between operations  1.31 us (1%)
    pallas_call x1, Pallas kernels, summed_over_devices(): pl.pallas_call(add_up, in_specs=[vmem], out_specs=vmem, out_shape=jax.Sha...  75.3 us
    pallas_call x1, Pallas kernels, encode_slots(): pl.pallas_call(body, in_specs=[pl.BlockSpec(memory_space=pltpu.SMEM), hbm...  51.2 us

profile of v4, /device:TPU:0, one launch (start us, length us, event | category | flops | bytes accessed | tf_op | source)
XLA Modules:
  0.0 129.5 jit_solution(9516345308140461697)
XLA Ops:
  1.3 51.2 %shard_map.222 = (bf16[8,96,4096]{2,1,0:T(8,128)(2,1)}, f32[768,128]{1,0:T(8,128)}) custom-call(s32[1]{0:T(128)S(6)} %copy.25.count_ref, bf16[8,48,4096]{2,1,0:T(8,128)(2,1)} %pix_hbm.1, bf16[8,96,4096]{2,1,0:T(8,128)(2,1)} %grad_hbm.1, bf16[48,96]{1,0:T(8,128)(2,1)} %bitcast.16, f32[1,96]{1,0:T(1,128)} %bitcast.17, f32[1,96]{1,0:T(1,128)} %bitcast.18, ...), custom_call_target="tpu_custom_call" | custom-call | tf_op jit(solution)/shard_map/pallas_call | solution.py:394
  52.5 75.3 %shard_map.223.full_ref = bf16[768,128]{1,0:T(8,128)(2,1)} custom-call(f32[768,128]{1,0:T(8,128)} %get-tuple-element.22.sums_ref), custom_call_target="tpu_custom_call" | custom-call | tf_op jit(solution)/shard_map/pallas_call | solution.py:513
  127.8 1.7 %shard_map.224 = (f32[48,96]{1,0:T(8,128)}, f32[1,96]{1,0:T(1,128)}, f32[1,96]{1,0:T(1,128)}, f32[49,96]{1,0:T(8,128)}, f32[1,96]{1,0:T(1,128)}, /*index=5*/f32[...) custom-call(bf16[768,128]{1,0:T(8,128)(2,1)} %shard_map.223.full_ref), custom_call_target="tpu_custom_call" | custom-call | tf_op jit(solution)/shard_map/pallas_call | solution.py:532
